TPU v7x, 32 devices: a whole 2x2x4 slice. The times are simulated.
32 devices in a mesh: depth: 8 (over z, y), rows: 4 (over x, core).
Axes of the slice: x: 2, y: 2, z: 4, core: 2. Of those that a mesh axis runs over, the one named last changes fastest.
Arguments:
- density: float32 [4, 256, 8192], P('rows', 'depth'), may hold values from 0.00078125 to 0.015625
- attenuation: float32 [4, 256, 8192], P('rows', 'depth'), may hold values from 0.00078125 to 0.015625
- measured: float32 [4, 4, 8192], P(None, 'rows'), may hold values from -3 to 3
- angle_ids: int32 [4], replicated, may hold values from 0 to 359
- sides: int32 [4], replicated, may hold values from 0 to 1, as said below
Outputs:
- grad_density: float32 [4, 256, 8192], P('rows', 'depth')
- grad_attenuation: float32 [4, 256, 8192], P('rows', 'depth')
Inputs may be any that keep to these rules, and one draw needn't show every extreme that they name: Half of the 4 views have sides 1.
All inputs are finite; a program needn't handle non-finite values.
Results may differ from a plain program's by a relative error of at most 0.0001.
Values sent between devices are 32-bit elements; how exact they have to be, the bound alone decides.
No kernel may reach another device: no remote copies, remote signals or barrier semaphores. Data moves between devices by JAX's collectives and lax.ppermute only.
A program may use at most 64 MiB of HBM per device.

v0:
```python
import jax
import jax.numpy as jnp
from jax import lax
from jax.sharding import PartitionSpec as P

ANGLES = 360


def entering(value, axis, join, neutral):
    count, mine = (lax.axis_size(axis), lax.axis_index(axis))
    pieces = lax.all_gather(value, axis)
    subtotal = jnp.full_like(value, 0) + jnp.asarray(neutral, value.dtype)

    def step(position, subtotal):
        longer = join(subtotal, pieces[position])
        return jnp.where(position < mine, longer, subtotal)

    return lax.fori_loop(0, count - 1, step, subtotal)


def with_halo(block, sides, width):
    for axis, dim in sides:
        count = lax.axis_size(axis)
        forward = [(i, i + 1) for i in range(count - 1)]
        backward = [(target, source) for source, target in forward]
        low = lax.ppermute(
            lax.slice_in_dim(block, block.shape[dim] - width, None, axis=dim), axis, forward
        )
        high = lax.ppermute(lax.slice_in_dim(block, 0, width, axis=dim), axis, backward)
        block = jnp.concatenate([low, block, high], axis=dim)
    return block


def tilt_angle(angle_ids):
    return 0.8 * jnp.sin(jnp.pi * (angle_ids.astype(jnp.float32) + 0.5) / ANGLES - jnp.pi / 2)


def shifted_pair(field):
    widths = [(0, 0)] * (field.ndim - 1)
    from_left = jnp.pad(field[..., :-1], widths + [(1, 0)])
    from_right = jnp.pad(field[..., 1:], widths + [(0, 1)])
    return (from_left, from_right)


def resample(field, tilting):
    from_left, from_right = shifted_pair(field)
    return (
        (1.0 - jnp.abs(tilting)) * field
        + jnp.maximum(tilting, 0.0) * from_left
        + jnp.maximum(-tilting, 0.0) * from_right
    )


def resample_back(field, tilting):
    from_left, from_right = shifted_pair(field)
    return (
        (1.0 - jnp.abs(tilting)) * field
        + jnp.maximum(tilting, 0.0) * from_right
        + jnp.maximum(-tilting, 0.0) * from_left
    )


def strict_cumsum(field):
    depth_cells = field.shape[2]
    row_ids = lax.broadcasted_iota(jnp.int32, (depth_cells, depth_cells), 0)
    col_ids = lax.broadcasted_iota(jnp.int32, (depth_cells, depth_cells), 1)
    strictly_lower = (row_ids > col_ids).astype(jnp.float32)
    return jnp.einsum("ij,vrjc->vric", strictly_lower, field, precision=lax.Precision.HIGHEST)


def combine_sum(earlier, later):
    return earlier + later


def prefix_total(slab_values):
    earlier = entering(slab_values, "depth", combine_sum, jnp.zeros_like(slab_values))
    overall = lax.psum(slab_values, "depth")
    return (earlier, overall)


def detector_blur(image):
    padded = with_halo(image, (("rows", 1),), 1)
    return 0.25 * padded[:, :-2] + 0.5 * padded[:, 1:-1] + 0.25 * padded[:, 2:]


def on_device(density, attenuation, measured, angle_ids, sides):
    grad_density = jnp.zeros(density.shape, jnp.float32)
    grad_attenuation = jnp.zeros(density.shape, jnp.float32)
    tilting = tilt_angle(angle_ids)[:, None, None, None]
    far_side = (sides == 1)[:, None, None, None]
    emission = resample(density[None], tilting)
    absorb = resample(attenuation[None], tilting)
    before_absorb = strict_cumsum(absorb)
    absorb_in, absorb_all = prefix_total(jnp.sum(absorb, axis=2))
    nearer_sum = absorb_in[:, :, None, :] + before_absorb
    depth_sum = jnp.where(far_side, absorb_all[:, :, None, :] - nearer_sum - absorb, nearer_sum)
    transmit = jnp.exp(-depth_sum)
    radiance = emission * transmit
    before_radiance = strict_cumsum(radiance)
    radiance_in, signal = prefix_total(jnp.sum(radiance, axis=2))
    residual = detector_blur(signal) - measured
    back_signal = detector_blur(residual)[:, :, None, :]
    emitted_before = radiance_in[:, :, None, :] + before_radiance
    behind = jnp.where(far_side, emitted_before, signal[:, :, None, :] - emitted_before - radiance)
    grad_density = grad_density + jnp.sum(resample_back(back_signal * transmit, tilting), axis=0)
    grad_attenuation = grad_attenuation + jnp.sum(
        resample_back(-back_signal * behind, tilting), axis=0
    )
    return (grad_density, grad_attenuation)


def solution(mesh):
    placed = (P("rows", "depth", None), P("rows", "depth", None), P(None, "rows", None), P(), P())
    return jax.shard_map(
        on_device,
        mesh=mesh,
        in_specs=placed,
        out_specs=(P("rows", "depth", None), P("rows", "depth", None)),
        check_vma=False,
    )
```

profile of v0, /device:TPU:1, one launch (start us, length us, event | category | flops | bytes accessed | tf_op | source)
XLA Modules:
  0.0 301.4 jit_solution(13441340693976916239)
XLA Ops:
  7.2 0.7 abs_subtract_fusion
  7.9 2.0 fusion.29
  9.9 0.3 pad_bitcast_fusion
  10.3 1.0 copy-done.3
  11.2 1.8 fusion.10
  13.0 1.6 fusion.28
  14.7 3.2 %pad_bitcast_fusion.2 = (f32[32,8192]{1,0:T(8,128)}, f32[32,8192]{1,0:T(8,128)}) fusion(f32[1,1,32,8191]{3,2,1,0:T(8,128)} %get-tuple-element.227, f32[1,1,32,8191]{3,2,1,0:T(8,128)} %get-tuple-element.226), kind=kLoop, calls=%fused_computation.36 | loop fusion | bytes 4194048 | tf_op jit(solution)/shard_map/mul | solution.py:50
  17.9 35.9 %all-gather.7.cloned.1.call-done = f32[8,4,8192]{2,1,0:T(4,128)} async-done(((f32[1,4,8192]{2,1,0:T(4,128)}), f32[8,4,8192]{2,1,0:T(4,128)}) %all-gather.7.cloned.1.call-update) | async-done | bytes 1048592 | tf_op jit(solution)/shard_map/all_gather | solution.py:11
  53.8 0.7 all-reduce.11.cloned.1.call-update
  54.6 8.0 %while.28 = (s32[]{:T(128)}, f32[4,1,8192]{2,1,0:T(1,128)S(1)}, s32[]{:T(128)}, f32[8,4,1,8192]{3,1,0,2:T(4,128)}, s32[]{:T(128)}, /*index=5*/s32[]{:T(128)}) while((s32[]{:T(128)}, f32[4,1,8192]{2,1,0:T(1,128)S(1)}, s32[]{:T(128)}, f32[8,4,1,8192]{3,1,0,2:T(4,128)}, s32[]{:T(128)}, /*index=5*/s32[]{:T(128)}) %tuple.91), condition=%wide.region_3.4_spmd.clone, body=%wide.region_2.3_spmd.clone.sunk | while | flops 98308 | bytes 655461 | solution.py:18
  54.6 0.9 constant_dynamic-slice_fusion.4
  55.5 0.2 broadcast_select_fusion.6
  55.8 0.9 constant_dynamic-slice_fusion.4
  56.7 0.2 broadcast_select_fusion.6
  56.9 0.9 constant_dynamic-slice_fusion.4
  57.8 0.2 broadcast_select_fusion.6
  58.1 0.9 constant_dynamic-slice_fusion.4
  59.2 0.9 constant_dynamic-slice_fusion.4
  60.4 0.9 constant_dynamic-slice_fusion.4
  61.5 0.9 constant_dynamic-slice_fusion.4
  62.7 64.2 %all-reduce.11.cloned.1.call-done = f32[4,8192]{1,0:T(4,128)} async-done(((f32[4,8192]{1,0:T(4,128)}), f32[4,8192]{1,0:T(4,128)}) %all-reduce.11.cloned.1.call-update) | async-done | bytes 131088 | tf_op jit(solution)/shard_map/psum | solution.py:77
  127.0 9.0 %fusion.24 = (f32[4,8192]{1,0:T(4,128)}, f32[4,1,32,8192]{3,2,0,1:T(8,128)}) fusion(f32[32,8192]{1,0:T(8,128)} %get-tuple-element.234, f32[4]{0:T(128)S(1)} %get-tuple-element.231, f32[32,8192]{1,0:T(8,128)} %get-tuple-element.235, f32[4]{0:T(128)S(1)} %get-tuple-element.230, f32[32,8192]{1,0:T(8,128)S(1)} %bitcast.82, f32[4]{0:T(128)S(1)} %get-tuple-element.220, ...), kind=kOutput, calls=%fused_computation.49 | convolution fusion | flops 425690112 | bytes 10879028 | tf_op jit(solution)/shard_map/ij,vrjc->vric/dot_general | solution.py:68
  136.0 39.7 %all-gather.9.cloned.1.call-done = f32[8,4,8192]{2,1,0:T(4,128)} async-done(((f32[1,4,8192]{2,1,0:T(4,128)}), f32[8,4,8192]{2,1,0:T(4,128)}) %all-gather.9.cloned.1.call-update) | async-done | bytes 1048592 | tf_op jit(solution)/shard_map/all_gather | solution.py:11
  175.7 0.6 all-reduce.13.cloned.1.call-update
  176.2 72.8 %all-reduce.13.cloned.1.call-done = f32[4,1,8192]{2,0,1:T(4,128)} async-done(((f32[4,1,8192]{2,0,1:T(4,128)}), f32[4,1,8192]{2,0,1:T(4,128)}) %all-reduce.13.cloned.1.call-update) | async-done | bytes 131088 | tf_op jit(solution)/shard_map/psum | solution.py:77
  249.1 4.4 %collective-permute-start.1 = (f32[4,1,8192]{2,0,1:T(4,128)}, f32[4,1,8192]{2,0,1:T(4,128)S(1)}, u32[]{:S(2)}, u32[]{:S(2)}) collective-permute-start(f32[4,1,8192]{2,0,1:T(4,128)} %all-reduce.13.cloned.1.call-done), channel_id=1, source_target_pairs={{1,0},{2,1},{3,2},{5,4},{6,5},{7,6},{9,8},{10,9},{11,10},{13,12},{... | collective-permute-start | bytes 393224 | tf_op jit(solution)/shard_map/ppermute | solution.py:29
  253.5 3.0 collective-permute-start
  256.5 0.9 collective-permute-done.1
  257.4 1.3 collective-permute-done
  258.8 1.0 copy_subtract_fusion
  259.8 1.9 collective-permute-start.3
  261.7 4.4 %collective-permute-start.2 = (f32[4,1,8192]{2,0,1:T(4,128)S(1)}, f32[4,1,8192]{2,0,1:T(4,128)S(1)}, u32[]{:S(2)}, u32[]{:S(2)}) collective-permute-start(f32[4,1,8192]{2,0,1:T(4,128)S(1)} %copy_subtract_fusion), channel_id=1, source_target_pairs={{0,1},{1,2},{2,3},{4,5},{5,6},{6,7},{8,9},{9,10},{10,11},{12,13},{... | collective-permute-start | bytes 393224 | tf_op jit(solution)/shard_map/ppermute | solution.py:26
  266.2 8.0 %while.29 = (s32[]{:T(128)}, f32[4,1,8192]{2,1,0:T(1,128)S(1)}, s32[]{:T(128)}, f32[8,4,1,8192]{3,1,0,2:T(4,128)}, s32[]{:T(128)}, /*index=5*/s32[]{:T(128)}) while((s32[]{:T(128)}, f32[4,1,8192]{2,1,0:T(1,128)S(1)}, s32[]{:T(128)}, f32[8,4,1,8192]{3,1,0,2:T(4,128)}, s32[]{:T(128)}, /*index=5*/s32[]{:T(128)}) %tuple.90), condition=%wide.region_8.9_spmd.clone, body=%wide.region_7.8_spmd.clone.sunk | while | flops 98308 | bytes 655461 | solution.py:18
  266.2 0.9 constant_dynamic-slice_fusion.5
  267.3 0.9 constant_dynamic-slice_fusion.5
  268.5 0.9 constant_dynamic-slice_fusion.5
  269.6 0.9 constant_dynamic-slice_fusion.5
  270.8 0.9 constant_dynamic-slice_fusion.5
  271.9 0.9 constant_dynamic-slice_fusion.5
  273.1 0.9 constant_dynamic-slice_fusion.5
  274.4 2.6 broadcast_multiply_fusion
  277.1 1.5 fusion.26
  278.5 0.7 copy-done
  279.2 0.3 copy-done.4
  279.5 0.3 copy-done.5
  279.8 5.0 %select_multiply_fusion = f32[4,1,32,8192]{3,2,0,1:T(8,128)S(1)} fusion(f32[4,8192]{1,0:T(4,128)S(1)} %bitcast.91, f32[4,8192]{1,0:T(4,128)S(1)} %get-tuple-element.218, pred[4]{0:T(512)(128)(4,1)S(1)} %broadcast_compare_fusion, f32[4,8192]{1,0:T(4,128)S(1)} %bitcast.92, f32[4,1,32,8192]{3,2,0,1:T(8,128)S(1)} %copy-done, f32[32,8192]{1,0:T(8,128)S(1)} %copy-done.4, ...), kind=kOutput, calls=%fused_computation.16 | convolution fusion | flops 420480000 | bytes 11927604 | tf_op jit(solution)/shard_map/ij,vrjc->vric/dot_general | solution.py:68
  284.8 3.5 %fusion.27 = (f32[4,1,32,8191]{3,2,0,1:T(8,128)S(1)}, f32[4,1,32,8191]{3,2,0,1:T(8,128)}) fusion(f32[4,1,32,8192]{3,2,0,1:T(8,128)S(1)} %select_multiply_fusion), kind=kLoop, calls=%fused_computation.52 | loop fusion | bytes 16775168 | tf_op jit(solution)/shard_map/slice | solution.py:41
  288.3 6.5 %add_reduce_fusion = (f32[32,8192]{1,0:T(8,128)}, f32[32,8192]{1,0:T(8,128)}) fusion(f32[4,1,32,8191]{3,2,0,1:T(8,128)} %get-tuple-element.225, f32[4,1,32,8191]{3,2,0,1:T(8,128)S(1)} %get-tuple-element.224, f32[4,1,32,8192]{3,2,0,1:T(8,128)S(1)} %select_multiply_fusion, f32[4]{0:T(128)S(1)} %get-tuple-element.231, f32[4]{0:T(128)S(1)} %get-tuple-element.230, ...), kind=kLoop, calls=%fused_computation.15 | loop fusion | flops 13107200 | bytes 27392048 | tf_op jit(solution)/shard_map/reduce_sum | solution.py:106
  (40 shorter events, 2.6 us)
Async XLA Ops:
  7.2 46.7 %all-gather.7.cloned.1.call-start = ((), (), s32[]{:S(2)}) async-start(), calls=%async_computation.2 | async-start | bytes 1179648 | tf_op jit(solution)/shard_map/all_gather | solution.py:11
  7.9 3.3 %copy-start.1 = (f32[1,32,8192]{2,1,0:T(8,128)S(1)}, f32[1,32,8192]{2,1,0:T(8,128)}, u32[]{:S(2)}) copy-start(f32[1,32,8192]{2,1,0:T(8,128)} %param.10) | copy-start | bytes 3145732
  9.9 3.1 %copy-start.2 = (f32[1,32,8192]{2,1,0:T(8,128)S(1)}, f32[1,32,8192]{2,1,0:T(8,128)}, u32[]{:S(2)}) copy-start(f32[1,32,8192]{2,1,0:T(8,128)} %param.9) | copy-start | bytes 3145732
  10.3 1.0 copy-start.3
  10.3 4.4 %copy-start.8 = (s32[4]{0:T(128)S(1)}, s32[4]{0:T(128)}, u32[]{:S(2)}) copy-start(s32[4]{0:T(128)} %param.13) | copy-start | bytes 52
  53.8 73.1 %all-reduce.11.cloned.1.call-start = ((), (), s32[]{:S(2)}) async-start(), calls=%async_computation | async-start | bytes 262144 | tf_op jit(solution)/shard_map/psum | solution.py:77
  54.6 121.1 %all-gather.9.cloned.1.call-start = ((), (), s32[]{:S(2)}) async-start(), calls=%async_computation.3 | async-start | bytes 1179648 | tf_op jit(solution)/shard_map/all_gather | solution.py:11
  127.0 131.8 %copy-start.6 = (f32[4,1,8192]{2,1,0:T(1,128)S(1)}, f32[4,1,8192]{2,1,0:T(1,128)}, u32[]{:S(2)}) copy-start(f32[4,1,8192]{2,1,0:T(1,128)} %param.11) | copy-start | bytes 393220
  175.7 73.4 %all-reduce.13.cloned.1.call-start = ((), (), s32[]{:S(2)}) async-start(), calls=%async_computation.1 | async-start | bytes 262144 | tf_op jit(solution)/shard_map/psum | solution.py:77
  249.1 8.4 %collective-permute-start.1 = (f32[4,1,8192]{2,0,1:T(4,128)}, f32[4,1,8192]{2,0,1:T(4,128)S(1)}, u32[]{:S(2)}, u32[]{:S(2)}) collective-permute-start(f32[4,1,8192]{2,0,1:T(4,128)} %all-reduce.13.cloned.1.call-done), channel_id=1, source_target_pairs={{1,0},{2,1},{3,2},{5,4},{6,5},{7,6},{9,8},{10,9},{11,10},{13,12},{... | collective-permute-start | bytes 393224 | tf_op jit(solution)/shard_map/ppermute | solution.py:29
  253.5 5.2 %collective-permute-start = (f32[4,1,8192]{2,0,1:T(4,128)}, f32[4,1,8192]{2,0,1:T(4,128)S(1)}, u32[]{:S(2)}, u32[]{:S(2)}) collective-permute-start(f32[4,1,8192]{2,0,1:T(4,128)} %all-reduce.13.cloned.1.call-done), channel_id=1, source_target_pairs={{0,1},{1,2},{2,3},{4,5},{5,6},{6,7},{8,9},{9,10},{10,11},{12,13},{... | collective-permute-start | bytes 393224 | tf_op jit(solution)/shard_map/ppermute | solution.py:26
  259.8 14.5 %collective-permute-start.3 = (f32[4,1,8192]{2,0,1:T(4,128)S(1)}, f32[4,1,8192]{2,0,1:T(4,128)S(1)}, u32[]{:S(2)}, u32[]{:S(2)}) collective-permute-start(f32[4,1,8192]{2,0,1:T(4,128)S(1)} %copy_subtract_fusion), channel_id=1, source_target_pairs={{1,0},{2,1},{3,2},{5,4},{6,5},{7,6},{9,8},{10,9},{11,10},{13,12},{... | collective-permute-start | bytes 393224 | tf_op jit(solution)/shard_map/ppermute | solution.py:29
  261.7 12.6 %collective-permute-start.2 = (f32[4,1,8192]{2,0,1:T(4,128)S(1)}, f32[4,1,8192]{2,0,1:T(4,128)S(1)}, u32[]{:S(2)}, u32[]{:S(2)}) collective-permute-start(f32[4,1,8192]{2,0,1:T(4,128)S(1)} %copy_subtract_fusion), channel_id=1, source_target_pairs={{0,1},{1,2},{2,3},{4,5},{5,6},{6,7},{8,9},{9,10},{10,11},{12,13},{... | collective-permute-start | bytes 393224 | tf_op jit(solution)/shard_map/ppermute | solution.py:26
  277.0 2.2 copy-start
  277.0 2.5 copy-start.4
  277.1 2.8 copy-start.5
  277.1 2.8 copy-start.7
Sparse Core Ops, SparseCore 0:
  13.1 40.6 all-gather.6
  58.0 68.9 all-reduce.10
  136.1 39.5 all-gather.8
  180.1 68.9 all-reduce.12
where the time goes:
time: 302 us; the launch traced here: 301 us
  waiting for transfers between devices  216 us (72%)
  local copies, waits for them, and re-layouts  27.4 us (9%)
  other arithmetic  15.5 us (5%)
  matrix products  14 us (5%)
  between operations  14 us (5%)
  starting transfers between devices  13.9 us (5%)
    psum x2, waiting for transfers between devices, prefix_total(): overall = lax.psum(slab_values, 'depth')  137 us
    all_gather x2, waiting for transfers between devices, entering(): pieces = lax.all_gather(value, axis)  75.6 us
    dot_general x2, matrix products, strict_cumsum(): jnp.einsum('ij,vrjc->vric', strictly_lower, field, precision=lax.Precisio...  14 us
    dynamic_slice x14, local copies, waits for them, and re-layouts, step(): longer = join(subtotal, pieces[position])  12.8 us
    ppermute x2, starting transfers between devices, with_halo(): lax.ppermute(lax.slice_in_dim(block, block.shape[dim] - width, None, axis...  7.42 us
    reduce_sum x1, other arithmetic, on_device(): jnp.sum(resample_back(-back_signal * behind, tilting), axis=0)  6.54 us
    ppermute x2, starting transfers between devices, with_halo(): lax.ppermute(lax.slice_in_dim(block, 0, width, axis=dim), axis, backward)  6.35 us
  transfers between devices with their start and end apart: 8, of which 6 were waited for; matrix products, arithmetic and copies ran while one was open for 7% of the time, Pallas kernels for 0%

commit v1 on v0

--- a/solution.py
+++ b/solution.py
@@ -74,7 +74,7 @@
 
 def prefix_total(slab_values):
     earlier = entering(slab_values, "depth", combine_sum, jnp.zeros_like(slab_values))
-    overall = lax.psum(slab_values, "depth")
+    overall = jnp.sum(lax.all_gather(slab_values, "depth"), axis=0)
     return (earlier, overall)
 
 

time: 302 us -> 166 us (0.55)
  waiting for transfers between devices: 216 us -> 77 us
    psum x2 -> x0, waiting for transfers between devices: 137 us -> none  [prefix_total(): overall = lax.psum(slab_values, 'depth')]
  transfers between devices with their start and end apart: 8 -> 6, of which waited for: 6 -> 4; matrix products, arithmetic and copies ran while one was open for 7% -> 8% of each run, Pallas kernels for 0% -> 0%
where the time goes in v1:
time: 166 us; the launch traced here: 165 us
  waiting for transfers between devices  77 us (46%)
  local copies, waits for them, and re-layouts  27.6 us (17%)
  other arithmetic  17.9 us (11%)
  between operations  14.3 us (9%)
  matrix products  14 us (8%)
  starting transfers between devices  13.8 us (8%)
    all_gather x2, waiting for transfers between devices, prefix_total(): overall = jnp.sum(lax.all_gather(slab_values, 'depth'), axis=0)  75 us
    dot_general x2, matrix products, strict_cumsum(): jnp.einsum('ij,vrjc->vric', strictly_lower, field, precision=lax.Precisio...  14 us
    dynamic_slice x14, local copies, waits for them, and re-layouts, step(): longer = join(subtotal, pieces[position])  12.8 us
    ppermute x2, starting transfers between devices, with_halo(): lax.ppermute(lax.slice_in_dim(block, block.shape[dim] - width, None, axis...  7.53 us
    reduce_sum x1, other arithmetic, on_device(): jnp.sum(resample_back(-back_signal * behind, tilting), axis=0)  6.54 us
    ppermute x2, starting transfers between devices, with_halo(): lax.ppermute(lax.slice_in_dim(block, 0, width, axis=dim), axis, backward)  6.2 us
    slice x2, local copies, waits for them, and re-layouts, shifted_pair(): from_right = jnp.pad(field[..., 1:], widths + [(0, 1)])  4.92 us
    slice x2, local copies, waits for them, and re-layouts, shifted_pair(): from_left = jnp.pad(field[..., :-1], widths + [(1, 0)])  3.62 us
  transfers between devices with their start and end apart: 6, of which 4 were waited for; matrix products, arithmetic and copies ran while one was open for 8% of the time, Pallas kernels for 0%

profile of v1, /device:TPU:1, one launch (start us, length us, event | category | flops | bytes accessed | tf_op | source)
XLA Modules:
  0.0 165.0 jit_solution(8506780430681044729)
XLA Ops:
  7.2 0.7 abs_subtract_fusion
  7.9 2.0 %fusion.33 = (f32[1,1,32,8191]{3,2,1,0:T(8,128)S(1)}, f32[1,1,32,8191]{3,2,1,0:T(8,128)S(1)}) fusion(f32[1,1,32,8192]{3,2,1,0:T(8,128)} %bitcast.76), kind=kLoop, calls=%fused_computation.61 | loop fusion | bytes 4193792 | tf_op jit(solution)/shard_map/slice | solution.py:40
  9.9 0.3 pad_bitcast_fusion
  10.3 1.0 copy-done.3
  11.3 1.8 %fusion.12 = f32[4,8192]{1,0:T(4,128)} fusion(f32[32,8192]{1,0:T(8,128)S(1)} %get-tuple-element.234, f32[32,8192]{1,0:T(8,128)S(1)} %get-tuple-element.235, f32[32,8192]{1,0:T(8,128)S(1)} %bitcast.77, f32[4]{0:T(128)S(1)} %get-tuple-element.229, f32[4]{0:T(128)S(1)} %get-tuple-element.228, f32[4]{0:T(128)S(1)} %get-tuple-element.218), kind=kLoop, calls=%fused_computation.25 | loop fusion | flops 6258688 | bytes 3276848 | tf_op jit(solution)/shard_map/reduce_sum | solution.py:94
  13.1 1.6 fusion.32
  14.8 3.2 %pad_bitcast_fusion.2 = (f32[32,8192]{1,0:T(8,128)}, f32[32,8192]{1,0:T(8,128)}) fusion(f32[1,1,32,8191]{3,2,1,0:T(8,128)} %get-tuple-element.225, f32[1,1,32,8191]{3,2,1,0:T(8,128)} %get-tuple-element.224), kind=kLoop, calls=%fused_computation.43 | loop fusion | bytes 4194048 | tf_op jit(solution)/shard_map/mul | solution.py:50
  17.9 35.9 %all-gather.7.cloned.1.call-done = f32[8,4,8192]{2,1,0:T(4,128)} async-done(((f32[1,4,8192]{2,1,0:T(4,128)}), f32[8,4,8192]{2,1,0:T(4,128)}) %all-gather.7.cloned.1.call-update) | async-done | bytes 1048592 | tf_op jit(solution)/shard_map/all_gather | solution.py:77
  53.8 8.0 %while.28 = (s32[]{:T(128)}, f32[4,1,8192]{2,1,0:T(1,128)S(1)}, s32[]{:T(128)}, f32[8,4,1,8192]{3,1,0,2:T(4,128)}, s32[]{:T(128)}, /*index=5*/s32[]{:T(128)}) while((s32[]{:T(128)}, f32[4,1,8192]{2,1,0:T(1,128)S(1)}, s32[]{:T(128)}, f32[8,4,1,8192]{3,1,0,2:T(4,128)}, s32[]{:T(128)}, /*index=5*/s32[]{:T(128)}) %tuple.86), condition=%wide.region_3.4_spmd.clone, body=%wide.region_2.3_spmd.clone.sunk | while | flops 98308 | bytes 655461 | solution.py:18
  53.8 0.9 constant_dynamic-slice_fusion.4
  54.8 0.2 broadcast_select_fusion.6
  55.0 0.9 constant_dynamic-slice_fusion.4
  55.9 0.2 broadcast_select_fusion.6
  56.1 0.9 constant_dynamic-slice_fusion.4
  57.0 0.2 broadcast_select_fusion.6
  57.3 0.9 constant_dynamic-slice_fusion.4
  58.4 0.9 constant_dynamic-slice_fusion.4
  59.6 0.9 constant_dynamic-slice_fusion.4
  60.7 0.9 constant_dynamic-slice_fusion.4
  62.0 1.4 reduce_sum.61
  63.4 9.0 %fusion.13 = (f32[4,8192]{1,0:T(4,128)}, f32[4,1,32,8192]{3,2,0,1:T(8,128)}) fusion(f32[32,8192]{1,0:T(8,128)} %get-tuple-element.232, f32[4]{0:T(128)S(1)} %get-tuple-element.229, f32[32,8192]{1,0:T(8,128)} %get-tuple-element.233, f32[4]{0:T(128)S(1)} %get-tuple-element.228, f32[32,8192]{1,0:T(8,128)S(1)} %bitcast.80, f32[4]{0:T(128)S(1)} %get-tuple-element.218, ...), kind=kOutput, calls=%fused_computation.27 | convolution fusion | flops 425690112 | bytes 10879028 | tf_op jit(solution)/shard_map/ij,vrjc->vric/dot_general | solution.py:68
  72.4 39.1 %all-gather.9.cloned.1.call-done = f32[8,4,8192]{2,1,0:T(4,128)} async-done(((f32[1,4,8192]{2,1,0:T(4,128)}), f32[8,4,8192]{2,1,0:T(4,128)}) %all-gather.9.cloned.1.call-update) | async-done | bytes 1048592 | tf_op jit(solution)/shard_map/all_gather | solution.py:77
  111.5 1.4 reduce_sum.63
  113.1 4.3 %collective-permute-start.1 = (f32[4,1,8192]{2,1,0:T(1,128)S(1)}, f32[4,1,8192]{2,1,0:T(1,128)S(1)}, u32[]{:S(2)}, u32[]{:S(2)}) collective-permute-start(f32[4,1,8192]{2,1,0:T(1,128)S(1)} %reduce_sum.64), channel_id=1, source_target_pairs={{1,0},{2,1},{3,2},{5,4},{6,5},{7,6},{9,8},{10,9},{11,10},{13,12},{... | collective-permute-start | bytes 393224 | tf_op jit(solution)/shard_map/ppermute | solution.py:29
  117.4 3.0 %collective-permute-start = (f32[4,1,8192]{2,1,0:T(1,128)S(1)}, f32[4,1,8192]{2,1,0:T(1,128)S(1)}, u32[]{:S(2)}, u32[]{:S(2)}) collective-permute-start(f32[4,1,8192]{2,1,0:T(1,128)S(1)} %reduce_sum.64), channel_id=1, source_target_pairs={{0,1},{1,2},{2,3},{4,5},{5,6},{6,7},{8,9},{9,10},{10,11},{12,13},{... | collective-permute-start | bytes 393224 | tf_op jit(solution)/shard_map/ppermute | solution.py:26
  120.4 0.7 collective-permute-done.1
  121.1 1.2 collective-permute-done
  122.3 0.3 add_subtract_fusion
  122.6 1.9 %collective-permute-start.3 = (f32[4,1,8192]{2,1,0:T(1,128)S(1)}, f32[4,1,8192]{2,1,0:T(1,128)S(1)}, u32[]{:S(2)}, u32[]{:S(2)}) collective-permute-start(f32[4,1,8192]{2,1,0:T(1,128)S(1)} %add_subtract_fusion), channel_id=1, source_target_pairs={{1,0},{2,1},{3,2},{5,4},{6,5},{7,6},{9,8},{10,9},{11,10},{13,12},{... | collective-permute-start | bytes 393224 | tf_op jit(solution)/shard_map/ppermute | solution.py:29
  124.5 4.5 %collective-permute-start.2 = (f32[4,1,8192]{2,1,0:T(1,128)S(1)}, f32[4,1,8192]{2,1,0:T(1,128)S(1)}, u32[]{:S(2)}, u32[]{:S(2)}) collective-permute-start(f32[4,1,8192]{2,1,0:T(1,128)S(1)} %add_subtract_fusion), channel_id=1, source_target_pairs={{0,1},{1,2},{2,3},{4,5},{5,6},{6,7},{8,9},{9,10},{10,11},{12,13},{... | collective-permute-start | bytes 393224 | tf_op jit(solution)/shard_map/ppermute | solution.py:26
  129.1 8.0 %while.29 = (s32[]{:T(128)}, f32[4,1,8192]{2,1,0:T(1,128)S(1)}, s32[]{:T(128)}, f32[8,4,1,8192]{3,1,0,2:T(4,128)}, s32[]{:T(128)}, /*index=5*/s32[]{:T(128)}) while((s32[]{:T(128)}, f32[4,1,8192]{2,1,0:T(1,128)S(1)}, s32[]{:T(128)}, f32[8,4,1,8192]{3,1,0,2:T(4,128)}, s32[]{:T(128)}, /*index=5*/s32[]{:T(128)}) %tuple.85), condition=%wide.region_8.9_spmd.clone, body=%wide.region_7.8_spmd.clone.sunk | while | flops 98308 | bytes 655461 | solution.py:18
  129.1 0.9 constant_dynamic-slice_fusion.5
  130.2 0.9 constant_dynamic-slice_fusion.5
  131.4 0.9 constant_dynamic-slice_fusion.5
  132.5 0.9 constant_dynamic-slice_fusion.5
  133.7 0.9 constant_dynamic-slice_fusion.5
  134.6 0.2 broadcast_select_fusion.7
  134.8 0.9 constant_dynamic-slice_fusion.5
  136.0 0.9 constant_dynamic-slice_fusion.5
  137.2 0.3 multiply_add_fusion.1
  137.7 2.6 %broadcast_multiply_fusion = f32[4,1,32,8192]{3,2,0,1:T(8,128)S(1)} fusion(f32[4,1,32,8192]{3,2,0,1:T(8,128)} %get-tuple-element.231, f32[4,8192]{1,0:T(4,128)S(1)} %bitcast.85), kind=kLoop, calls=%fused_computation.28 | loop fusion | flops 1048576 | bytes 8519680 | tf_op jit(solution)/shard_map/mul | solution.py:105
  140.3 1.5 fusion.30
  141.8 0.7 copy-done
  142.5 0.3 copy-done.4
  142.8 0.3 copy-done.5
  143.1 5.0 %select_multiply_fusion = f32[4,1,32,8192]{3,2,0,1:T(8,128)S(1)} fusion(f32[4,1,32,8192]{3,2,0,1:T(8,128)S(1)} %copy-done, f32[4,8192]{1,0:T(4,128)S(1)} %reduce_sum.63, f32[4,8192]{1,0:T(4,128)S(1)} %bitcast.90, f32[4,8192]{1,0:T(4,128)S(1)} %fusion.29, f32[32,8192]{1,0:T(8,128)S(1)} %copy-done.4, f32[4]{0:T(128)S(1)} %get-tuple-element.229, ...), kind=kOutput, calls=%fused_computation.16 | convolution fusion | flops 420480000 | bytes 11927604 | tf_op jit(solution)/shard_map/ij,vrjc->vric/dot_general | solution.py:68
  148.1 3.5 %fusion.31 = (f32[4,1,32,8191]{3,2,0,1:T(8,128)S(1)}, f32[4,1,32,8191]{3,2,0,1:T(8,128)}) fusion(f32[4,1,32,8192]{3,2,0,1:T(8,128)S(1)} %select_multiply_fusion), kind=kLoop, calls=%fused_computation.59 | loop fusion | bytes 16775168 | tf_op jit(solution)/shard_map/slice | solution.py:41
  151.6 6.5 %add_reduce_fusion = (f32[32,8192]{1,0:T(8,128)}, f32[32,8192]{1,0:T(8,128)}) fusion(f32[4,1,32,8191]{3,2,0,1:T(8,128)} %get-tuple-element.223, f32[4,1,32,8191]{3,2,0,1:T(8,128)S(1)} %get-tuple-element.222, f32[4,1,32,8192]{3,2,0,1:T(8,128)S(1)} %select_multiply_fusion, f32[4]{0:T(128)S(1)} %get-tuple-element.229, f32[4]{0:T(128)S(1)} %get-tuple-element.228, ...), kind=kLoop, calls=%fused_computation.15 | loop fusion | flops 13107200 | bytes 27392048 | tf_op jit(solution)/shard_map/reduce_sum | solution.py:106
  (37 shorter events, 2.6 us)
Async XLA Ops:
  7.2 46.7 %all-gather.7.cloned.1.call-start = ((), (), s32[]{:S(2)}) async-start(), calls=%async_computation | async-start | bytes 1179648 | tf_op jit(solution)/shard_map/all_gather | solution.py:77
  7.9 3.3 %copy-start.1 = (f32[1,32,8192]{2,1,0:T(8,128)S(1)}, f32[1,32,8192]{2,1,0:T(8,128)}, u32[]{:S(2)}) copy-start(f32[1,32,8192]{2,1,0:T(8,128)} %param.10) | copy-start | bytes 3145732
  9.9 3.2 %copy-start.2 = (f32[1,32,8192]{2,1,0:T(8,128)S(1)}, f32[1,32,8192]{2,1,0:T(8,128)}, u32[]{:S(2)}) copy-start(f32[1,32,8192]{2,1,0:T(8,128)} %param.9) | copy-start | bytes 3145732
  10.3 1.0 copy-start.3
  10.3 4.5 %copy-start.7 = (s32[4]{0:T(128)S(1)}, s32[4]{0:T(128)}, u32[]{:S(2)}) copy-start(s32[4]{0:T(128)} %param.13) | copy-start | bytes 52
  13.0 98.5 %all-gather.9.cloned.1.call-start = ((), (), s32[]{:S(2)}) async-start(), calls=%async_computation.1 | async-start | bytes 1179648 | tf_op jit(solution)/shard_map/all_gather | solution.py:77
  63.4 58.9 %copy-start.6 = (f32[4,1,8192]{2,1,0:T(1,128)S(1)}, f32[4,1,8192]{2,1,0:T(1,128)}, u32[]{:S(2)}) copy-start(f32[4,1,8192]{2,1,0:T(1,128)} %param.11) | copy-start | bytes 393220
  113.1 8.0 %collective-permute-start.1 = (f32[4,1,8192]{2,1,0:T(1,128)S(1)}, f32[4,1,8192]{2,1,0:T(1,128)S(1)}, u32[]{:S(2)}, u32[]{:S(2)}) collective-permute-start(f32[4,1,8192]{2,1,0:T(1,128)S(1)} %reduce_sum.64), channel_id=1, source_target_pairs={{1,0},{2,1},{3,2},{5,4},{6,5},{7,6},{9,8},{10,9},{11,10},{13,12},{... | collective-permute-start | bytes 393224 | tf_op jit(solution)/shard_map/ppermute | solution.py:29
  117.4 4.9 %collective-permute-start = (f32[4,1,8192]{2,1,0:T(1,128)S(1)}, f32[4,1,8192]{2,1,0:T(1,128)S(1)}, u32[]{:S(2)}, u32[]{:S(2)}) collective-permute-start(f32[4,1,8192]{2,1,0:T(1,128)S(1)} %reduce_sum.64), channel_id=1, source_target_pairs={{0,1},{1,2},{2,3},{4,5},{5,6},{6,7},{8,9},{9,10},{10,11},{12,13},{... | collective-permute-start | bytes 393224 | tf_op jit(solution)/shard_map/ppermute | solution.py:26
  122.6 14.6 %collective-permute-start.3 = (f32[4,1,8192]{2,1,0:T(1,128)S(1)}, f32[4,1,8192]{2,1,0:T(1,128)S(1)}, u32[]{:S(2)}, u32[]{:S(2)}) collective-permute-start(f32[4,1,8192]{2,1,0:T(1,128)S(1)} %add_subtract_fusion), channel_id=1, source_target_pairs={{1,0},{2,1},{3,2},{5,4},{6,5},{7,6},{9,8},{10,9},{11,10},{13,12},{... | collective-permute-start | bytes 393224 | tf_op jit(solution)/shard_map/ppermute | solution.py:29
  124.5 12.7 %collective-permute-start.2 = (f32[4,1,8192]{2,1,0:T(1,128)S(1)}, f32[4,1,8192]{2,1,0:T(1,128)S(1)}, u32[]{:S(2)}, u32[]{:S(2)}) collective-permute-start(f32[4,1,8192]{2,1,0:T(1,128)S(1)} %add_subtract_fusion), channel_id=1, source_target_pairs={{0,1},{1,2},{2,3},{4,5},{5,6},{6,7},{8,9},{9,10},{10,11},{12,13},{... | collective-permute-start | bytes 393224 | tf_op jit(solution)/shard_map/ppermute | solution.py:26
  140.3 2.2 %copy-start = (f32[4,1,32,8192]{3,2,0,1:T(8,128)S(1)}, f32[4,1,32,8192]{3,2,0,1:T(8,128)}, u32[]{:S(2)}) copy-start(f32[4,1,32,8192]{3,2,0,1:T(8,128)} %get-tuple-element.231) | copy-start | bytes 12582916
  140.3 2.5 %copy-start.4 = (f32[32,8192]{1,0:T(8,128)S(1)}, f32[32,8192]{1,0:T(8,128)}, u32[]{:S(2)}) copy-start(f32[32,8192]{1,0:T(8,128)} %get-tuple-element.232) | copy-start | bytes 3145732
  140.3 2.8 %copy-start.5 = (f32[32,8192]{1,0:T(8,128)S(1)}, f32[32,8192]{1,0:T(8,128)}, u32[]{:S(2)}) copy-start(f32[32,8192]{1,0:T(8,128)} %get-tuple-element.233) | copy-start | bytes 3145732
Sparse Core Ops, SparseCore 0:
  13.2 40.6 all-gather.6
  72.5 38.9 all-gather.8
